TPU v7x, 256 devices: a whole 4x4x8 slice. The times are simulated.
256 devices in a mesh: section: 2 (over core), dp: 32 (over z, x), mp: 4 (over y).
Axes of the slice: x: 4, y: 4, z: 8, core: 2. Of those that a mesh axis runs over, the one named last changes fastest.
Arguments:
- features: bfloat16 [32768, 4096], P(('section', 'dp'), 'mp'), may hold values from -16 to 16
- w_in: bfloat16 [4096, 2048], P(('section', 'dp'), 'mp'), may hold values from -0.09375 to 0.09375
- w_out: bfloat16 [512, 2048], P(('section', 'dp'), 'mp'), may hold values from -0.125 to 0.125
- codebook: bfloat16 [3, 65536, 512], P(None, ('section', 'dp'), 'mp'), may hold values from -3 to 3
- codes: int32 [3, 32768], P(None, ('section', 'dp')), may hold values from 0 to 65535, as said below
- decoder_grad: bfloat16 [32768, 512], P(('section', 'dp'), 'mp'), may hold values from -16 to 16
Outputs:
- in_grad: float32 [4096, 2048], P(('section', 'dp'), 'mp')
- out_grad: float32 [512, 2048], P(('section', 'dp'), 'mp')
- code_sums: float32 [3, 65536, 512], P(None, ('section', 'dp'), 'mp')
Inputs may be any that keep to these rules, and one draw needn't show every extreme that they name: Row k of a level's codebook belongs to owner k // 1024. Within the 512 items of one device (aligned blocks of items), at each level at most 16 codes belong to one owner; at each level some owner receives exactly 16 codes from every device's items.
All inputs are finite; a program needn't handle non-finite values.
Results may differ from a plain program's by a relative error of at most 0.0026.
Values may be sent and summed in bfloat16 or wider, within the bound.
No kernel may reach another device: no remote copies, remote signals or barrier semaphores. Data moves between devices by JAX's collectives and lax.ppermute only.
A program may use at most 64 MiB of HBM per device.

v0:
```python
import jax
import jax.numpy as jnp
from jax import lax
from jax.sharding import PartitionSpec as P

BETA = 0.25


def silu_slope(preact):
    logistic = jax.nn.sigmoid(preact)
    return logistic * (1.0 + preact * (1.0 - logistic))


def send_requests(outgoing):
    return lax.all_to_all(outgoing, ("section", "dp"), split_axis=0, concat_axis=0, tiled=True)


def send_rows(outgoing):
    return lax.all_to_all(outgoing, ("section", "dp"), split_axis=0, concat_axis=0, tiled=True)


def send_sums(outgoing):
    return lax.all_to_all(outgoing, ("section", "dp"), split_axis=0, concat_axis=0, tiled=True)


def shards(features, w_in, w_out, codebook, codes, decoder_grad):
    owners = lax.axis_size(("section", "dp"))
    item_rows = features.shape[0]
    levels, rows_own, width_part = codebook.shape
    capacity = max(2, 2 * item_rows // owners)
    items_all = item_rows * owners
    all_features = lax.all_gather(features, "mp", axis=1, tiled=True)
    preact = jnp.dot(
        all_features,
        lax.all_gather(w_in, ("section", "dp"), axis=0, tiled=True),
        preferred_element_type=jnp.float32,
    )
    hidden = jax.nn.silu(preact).astype(jnp.bfloat16)
    out_full = lax.all_gather(w_out, ("section", "dp"), axis=0, tiled=True)
    latent_part = lax.dot_general(
        hidden, out_full, (((1,), (1,)), ((), ())), preferred_element_type=jnp.float32
    )
    latent = lax.psum_scatter(latent_part, "mp", scatter_dimension=1, tiled=True)
    owner_of = codes // rows_own
    level_ids = jnp.arange(levels, dtype=jnp.int32)[:, None]
    flat_rows = codes % rows_own + level_ids * rows_own
    matches = (owner_of[:, :, None] == jnp.arange(owners, dtype=jnp.int32)).astype(jnp.int32)
    ranking = jnp.sum(jnp.cumsum(matches, axis=1) * matches, axis=2) - 1
    flat_book = codebook.reshape(levels * rows_own, width_part)
    slot_of = owner_of * capacity + ranking
    requests = (
        jnp.zeros((levels, owners * capacity), jnp.int32).at[level_ids, slot_of].set(flat_rows)
    )
    asked_list = []
    fetched_list = []
    for level_index in range(levels):
        asked_rows = send_requests(requests[level_index].reshape(owners, capacity))
        rows_back = send_rows(jnp.take(flat_book, asked_rows, axis=0))
        asked_list.append(asked_rows)
        fetched_list.append(
            jnp.take(rows_back.reshape(owners * capacity, width_part), slot_of[level_index], axis=0)
        )
    codewords = jnp.stack(fetched_list)
    residual = latent
    pull_sum = jnp.zeros_like(latent)
    inputs = []
    for level_index in range(levels):
        inputs.append(residual)
        residual = residual - codewords[level_index].astype(jnp.float32)
        pull_sum = pull_sum + residual
    code_total = jnp.zeros((levels * rows_own, width_part), jnp.float32)
    for level_index in range(levels):
        outgoing = (
            jnp.zeros((owners * capacity, width_part), jnp.float32)
            .at[slot_of[level_index]]
            .set(inputs[level_index])
        )
        incoming = send_sums(outgoing.reshape(owners, capacity, width_part))
        code_total = code_total.at[asked_list[level_index].reshape(-1)].add(
            incoming.reshape(-1, width_part)
        )
    code_sums = code_total.reshape(levels, rows_own, width_part)
    latent_grad = (
        (decoder_grad.astype(jnp.float32) + 2.0 * BETA * pull_sum)
        / jnp.sqrt(jnp.float32(items_all))
    ).astype(jnp.bfloat16)
    grad_full = lax.all_gather(latent_grad, "mp", axis=1, tiled=True)
    out_grad = lax.psum_scatter(
        lax.dot_general(
            grad_full, hidden, (((0,), (0,)), ((), ())), preferred_element_type=jnp.float32
        ),
        ("section", "dp"),
        scatter_dimension=0,
        tiled=True,
    )
    back_hidden = jnp.dot(grad_full, out_full, preferred_element_type=jnp.float32)
    pre_grad = (back_hidden * silu_slope(preact)).astype(jnp.bfloat16)
    in_grad = lax.psum_scatter(
        lax.dot_general(
            all_features, pre_grad, (((0,), (0,)), ((), ())), preferred_element_type=jnp.float32
        ),
        ("section", "dp"),
        scatter_dimension=0,
        tiled=True,
    )
    return (in_grad, out_grad, code_sums)


def solution(mesh):
    in_specs = (
        P(("section", "dp"), "mp"),
        P(("section", "dp"), "mp"),
        P(("section", "dp"), "mp"),
        P(None, ("section", "dp"), "mp"),
        P(None, ("section", "dp")),
        P(("section", "dp"), "mp"),
    )
    out_specs = (
        P(("section", "dp"), "mp"),
        P(("section", "dp"), "mp"),
        P(None, ("section", "dp"), "mp"),
    )
    return jax.shard_map(shards, mesh=mesh, in_specs=in_specs, out_specs=out_specs, check_vma=False)
```

profile of v0, /device:TPU:8, one launch (start us, length us, event | category | flops | bytes accessed | tf_op | source)
XLA Modules:
  0.0 587.1 jit_solution(6716186569917230961)
XLA Ops:
  9.5 3.6 reduce-window.6
  15.3 6.2 %scatter_custom_fusion.6 = s32[3072]{0:T(1024)S(1)} fusion(s32[1536]{0:T(1024)S(1)} %reshape.377, s32[1536]{0:T(1024)S(1)} %reshape.379, s32[]{:T(128)} %constant.45.clone.1), kind=kCustom, calls=%fused_computation.72 | custom fusion | bytes 12292
  22.2 11.9 %all-to-all-start.2 = ((s32[64,1,16]{2,1,0:T(1,128)}), s32[64,1,16]{2,1,0:T(1,128)S(1)}, u32[]{:S(2)}, u32[]{:S(2)}) async-start(s32[64,1,16]{2,1,0:T(1,128)} %bitcast.9), calls=%async_computation.3 | async-start | bytes 65536 | tf_op jit(solution)/shard_map/all_to_all | solution.py:15
  34.2 129.8 %all_gather.14 = bf16[512,512]{1,0:T(8,128)(2,1)S(1)} all-gather(bf16[8,512]{1,0:T(8,128)(2,1)} %param.12), channel_id=1, replica_groups=mesh['section'=2,'dp'=32,'mp'=4] {'section','dp'}, dimensions={0}, use_global_device_ids=true | all-gather | bytes 532480 | tf_op jit(solution)/shard_map/all_gather | solution.py:39
  165.5 19.5 %all-to-all-start.4 = ((s32[64,1,16]{2,1,0:T(1,128)}), s32[64,1,16]{2,1,0:T(1,128)S(1)}, u32[]{:S(2)}, u32[]{:S(2)}) async-start(s32[64,1,16]{2,1,0:T(1,128)} %bitcast.14), calls=%async_computation.5 | async-start | bytes 65536 | tf_op jit(solution)/shard_map/all_to_all | solution.py:15
  185.1 9.1 %all-to-all-done.4 = s32[64,1,16]{2,1,0:T(1,128)S(1)} async-done(((s32[64,1,16]{2,1,0:T(1,128)}), s32[64,1,16]{2,1,0:T(1,128)S(1)}, u32[]{:S(2)}, u32[]{:S(2)}) %all-to-all-start.4) | async-done | bytes 4128 | tf_op jit(solution)/shard_map/all_to_all | solution.py:15
  194.2 4.6 all-to-all-start
  198.9 3.2 gather_fusion.4
  203.1 6.8 %multiply_convert_fusion = (bf16[512,512]{1,0:T(8,128)(2,1)S(1)}, f32[512,512]{1,0:T(8,128)}) fusion(bf16[512,4096]{1,0:T(8,128)(2,1)} %all-gather.3.cloned.1.call-done, bf16[4096,512]{1,0:T(8,128)(2,1)} %all-gather.5.cloned.1.call-done), kind=kOutput, calls=%fused_computation.20 | convolution fusion | flops 2148794368 | bytes 9961472 | tf_op jit(solution)/shard_map/dot_general | solution.py:33
  211.4 10.2 %all-to-all-start.5 = ((bf16[64,16,128]{2,1,0:T(8,128)(2,1)}), bf16[64,16,128]{2,1,0:T(8,128)(2,1)S(1)}, u32[]{:S(2)}, u32[]{:S(2)}) async-start(bf16[64,16,128]{2,1,0:T(8,128)(2,1)} %broadcast_select_fusion), calls=%async_computation.6 | async-start | bytes 524288 | tf_op jit(solution)/shard_map/all_to_all | solution.py:19
  221.7 3.2 gather_fusion.2
  225.9 7.6 %all-to-all-done.5 = bf16[64,16,128]{2,1,0:T(8,128)(2,1)S(1)} async-done(((bf16[64,16,128]{2,1,0:T(8,128)(2,1)}), bf16[64,16,128]{2,1,0:T(8,128)(2,1)S(1)}, u32[]{:S(2)}, u32[]{:S(2)}) %all-to-all-start.5) | async-done | bytes 262176 | tf_op jit(solution)/shard_map/all_to_all | solution.py:19
  233.5 6.0 %all-to-all-start.3 = ((bf16[64,16,128]{2,1,0:T(8,128)(2,1)}), bf16[64,16,128]{2,1,0:T(8,128)(2,1)S(1)}, u32[]{:S(2)}, u32[]{:S(2)}) async-start(bf16[64,16,128]{2,1,0:T(8,128)(2,1)} %broadcast_select_fusion.1), calls=%async_computation.4 | async-start | bytes 524288 | tf_op jit(solution)/shard_map/all_to_all | solution.py:19
  239.5 3.2 gather_fusion
  243.6 7.7 %all-to-all-done.3 = bf16[64,16,128]{2,1,0:T(8,128)(2,1)S(1)} async-done(((bf16[64,16,128]{2,1,0:T(8,128)(2,1)}), bf16[64,16,128]{2,1,0:T(8,128)(2,1)S(1)}, u32[]{:S(2)}, u32[]{:S(2)}) %all-to-all-start.3) | async-done | bytes 262176 | tf_op jit(solution)/shard_map/all_to_all | solution.py:19
  251.4 6.0 %all-to-all-start.1 = ((bf16[64,16,128]{2,1,0:T(8,128)(2,1)}), bf16[64,16,128]{2,1,0:T(8,128)(2,1)S(1)}, u32[]{:S(2)}, u32[]{:S(2)}) async-start(bf16[64,16,128]{2,1,0:T(8,128)(2,1)} %broadcast_select_fusion.2), calls=%async_computation.2 | async-start | bytes 524288 | tf_op jit(solution)/shard_map/all_to_all | solution.py:19
  260.3 8.9 %all-to-all-done.1 = bf16[64,16,128]{2,1,0:T(8,128)(2,1)S(1)} async-done(((bf16[64,16,128]{2,1,0:T(8,128)(2,1)}), bf16[64,16,128]{2,1,0:T(8,128)(2,1)S(1)}, u32[]{:S(2)}, u32[]{:S(2)}) %all-to-all-start.1) | async-done | bytes 262176 | tf_op jit(solution)/shard_map/all_to_all | solution.py:19
  271.8 14.5 %all_gather.15 = bf16[512,512]{1,0:T(8,128)(2,1)S(1)} all-gather(bf16[512,128]{1,0:T(8,128)(2,1)S(1)} %multiply_convert_fusion.1), channel_id=1, replica_groups=mesh['section'=2,'dp'=32,'mp'=4] {'mp'}, dimensions={1}, use_global_device_ids=true | all-gather | bytes 655360 | tf_op jit(solution)/shard_map/all_gather | solution.py:87
  287.8 8.6 %convolution_bitcast_fusion = f32[4096,512]{0,1:T(8,128)} fusion(bf16[512,4096]{1,0:T(8,128)(2,1)} %all-gather.3.cloned.1.call-done, bf16[512,512]{1,0:T(8,128)(2,1)S(1)} %all_gather.15, bf16[512,512]{1,0:T(8,128)(2,1)S(1)} %all_gather.14, f32[512,512]{1,0:T(8,128)} %get-tuple-element.28), kind=kOutput, calls=%fused_computation.13 | convolution fusion | flops 2418278400 | bytes 14680064 | tf_op jit(solution)/shard_map/dot_general | solution.py:99
  296.4 9.0 %copy.17 = f32[4096,512]{1,0:T(8,128)} copy(f32[4096,512]{0,1:T(8,128)} %convolution_bitcast_fusion) | data formatting | bytes 16777216
  306.4 2.7 scatter_custom_fusion.2
  309.1 5.9 %all-to-all-start.7 = ((f32[64,16,128]{2,1,0:T(8,128)}), f32[64,16,128]{2,1,0:T(8,128)S(1)}, u32[]{:S(2)}, u32[]{:S(2)}) async-start(f32[64,16,128]{2,1,0:T(8,128)} %bitcast.27), calls=%async_computation.9 | async-start | bytes 1048576 | tf_op jit(solution)/shard_map/all_to_all | solution.py:23
  317.5 14.3 %all-to-all-done.7 = f32[64,16,128]{2,1,0:T(8,128)S(1)} async-done(((f32[64,16,128]{2,1,0:T(8,128)}), f32[64,16,128]{2,1,0:T(8,128)S(1)}, u32[]{:S(2)}, u32[]{:S(2)}) %all-to-all-start.7) | async-done | bytes 524320 | tf_op jit(solution)/shard_map/all_to_all | solution.py:23
  331.8 6.6 %all-to-all-start.6 = ((f32[64,16,128]{2,1,0:T(8,128)}), f32[64,16,128]{2,1,0:T(8,128)S(1)}, u32[]{:S(2)}, u32[]{:S(2)}) async-start(f32[64,16,128]{2,1,0:T(8,128)} %bitcast.22), calls=%async_computation.8 | async-start | bytes 1048576 | tf_op jit(solution)/shard_map/all_to_all | solution.py:23
  338.4 2.7 scatter_custom_fusion.4
  341.1 14.1 %all-to-all-done.6 = f32[64,16,128]{2,1,0:T(8,128)S(1)} async-done(((f32[64,16,128]{2,1,0:T(8,128)}), f32[64,16,128]{2,1,0:T(8,128)S(1)}, u32[]{:S(2)}, u32[]{:S(2)}) %all-to-all-start.6) | async-done | bytes 524320 | tf_op jit(solution)/shard_map/all_to_all | solution.py:23
  355.2 6.8 %all-to-all-start.8 = ((f32[64,16,128]{2,1,0:T(8,128)}), f32[64,16,128]{2,1,0:T(8,128)S(1)}, u32[]{:S(2)}, u32[]{:S(2)}) async-start(f32[64,16,128]{2,1,0:T(8,128)} %bitcast.32), calls=%async_computation.10 | async-start | bytes 1048576 | tf_op jit(solution)/shard_map/all_to_all | solution.py:23
  365.0 6.8 %scatter_custom_fusion.1 = f32[3072,128]{1,0:T(8,128)S(1)} fusion(s32[1024]{0:T(1024)S(1)} %bitcast.95, f32[1024,128]{1,0:T(8,128)} %bitcast.80, f32[]{:T(128)} %constant.79.clone.1), kind=kCustom, calls=%fused_computation.22 | custom fusion | flops 131072 | bytes 1573376 | tf_op jit(solution)/shard_map/scatter-add | solution.py:79
  371.8 6.6 %scatter_fusion = f32[3072,128]{1,0:T(8,128)S(1)} fusion(f32[3072,128]{1,0:T(8,128)S(1)} %scatter_custom_fusion.1, s32[1024]{0:T(1024)S(1)} %bitcast.94, f32[1024,128]{1,0:T(8,128)S(1)} %bitcast.75), kind=kCustom, calls=%fused_computation.9 | custom fusion | flops 131072 | bytes 1576960 | tf_op jit(solution)/shard_map/scatter-add | solution.py:79
  380.0 6.6 %scatter_fusion.1 = f32[3072,128]{1,0:T(8,128)S(1)} fusion(f32[3072,128]{1,0:T(8,128)S(1)} %scatter_fusion, s32[1024]{0:T(1024)S(1)} %bitcast.93, f32[1024,128]{1,0:T(8,128)S(1)} %bitcast.76), kind=kCustom, calls=%fused_computation.11 | custom fusion | flops 131072 | bytes 1576960 | tf_op jit(solution)/shard_map/scatter-add | solution.py:79
  386.6 38.4 %reduce-scatter.8.cloned.1.call-done = f32[8,512]{1,0:T(8,128)} async-done(((f32[512,512]{1,0:T(8,128)}), f32[8,512]{1,0:T(8,128)}) %reduce-scatter.8.cloned.1.call-update) | async-done | bytes 16400 | tf_op jit(solution)/shard_map/reduce_scatter | solution.py:88
  425.0 155.6 %reduce-scatter.10.cloned.1.call-done = f32[64,512]{1,0:T(8,128)} async-done(((f32[4096,512]{1,0:T(8,128)}), f32[64,512]{1,0:T(8,128)}) %reduce-scatter.10.cloned.1.call-update) | async-done | bytes 131088
  (87 shorter events, 26.1 us)
Async XLA Ops:
  7.2 191.8 %copy-start = (bf16[3,1024,128]{2,1,0:T(8,128)(2,1)S(1)}, bf16[3,1024,128]{2,1,0:T(8,128)(2,1)}, u32[]{:S(2)}) copy-start(bf16[3,1024,128]{2,1,0:T(8,128)(2,1)} %param.13) | copy-start | bytes 2359300
  7.2 195.9 %all-gather.3.cloned.1.call-start = ((), (), s32[]{:S(2)}) async-start(), calls=%async_computation.12 | async-start | bytes 5242880 | tf_op jit(solution)/shard_map/all_gather | solution.py:32
  7.9 195.2 %all-gather.5.cloned.1.call-start = ((), (), s32[]{:S(2)}) async-start(), calls=%async_computation.13 | async-start | bytes 4259840 | tf_op jit(solution)/shard_map/all_gather | solution.py:35
  22.2 143.2 %all-to-all-start.2 = ((s32[64,1,16]{2,1,0:T(1,128)}), s32[64,1,16]{2,1,0:T(1,128)S(1)}, u32[]{:S(2)}, u32[]{:S(2)}) async-start(s32[64,1,16]{2,1,0:T(1,128)} %bitcast.9), calls=%async_computation.3 | async-start | bytes 65536 | tf_op jit(solution)/shard_map/all_to_all | solution.py:15
  165.5 28.8 %all-to-all-start.4 = ((s32[64,1,16]{2,1,0:T(1,128)}), s32[64,1,16]{2,1,0:T(1,128)S(1)}, u32[]{:S(2)}, u32[]{:S(2)}) async-start(s32[64,1,16]{2,1,0:T(1,128)} %bitcast.14), calls=%async_computation.5 | async-start | bytes 65536 | tf_op jit(solution)/shard_map/all_to_all | solution.py:15
  194.2 17.2 %all-to-all-start = ((s32[64,1,16]{2,1,0:T(1,128)}), s32[64,1,16]{2,1,0:T(1,128)S(1)}, u32[]{:S(2)}, u32[]{:S(2)}) async-start(s32[64,1,16]{2,1,0:T(1,128)} %bitcast.3), calls=%async_computation.1 | async-start | bytes 65536 | tf_op jit(solution)/shard_map/all_to_all | solution.py:15
  198.8 71.8 %reduce-scatter.6.cloned.1.call-start = ((), (), s32[]{:S(2)}) async-start(), calls=%async_computation.14 | async-start | bytes 1310720 | tf_op jit(solution)/shard_map/reduce_scatter | solution.py:43
  211.4 22.1 %all-to-all-start.5 = ((bf16[64,16,128]{2,1,0:T(8,128)(2,1)}), bf16[64,16,128]{2,1,0:T(8,128)(2,1)S(1)}, u32[]{:S(2)}, u32[]{:S(2)}) async-start(bf16[64,16,128]{2,1,0:T(8,128)(2,1)} %broadcast_select_fusion), calls=%async_computation.6 | async-start | bytes 524288 | tf_op jit(solution)/shard_map/all_to_all | solution.py:19
  224.9 45.7 %copy-start.4 = (bf16[512,128]{1,0:T(8,128)(2,1)S(1)}, bf16[512,128]{1,0:T(8,128)(2,1)}, u32[]{:S(2)}) copy-start(bf16[512,128]{1,0:T(8,128)(2,1)} %param.15) | copy-start | bytes 393220
  233.5 17.9 %all-to-all-start.3 = ((bf16[64,16,128]{2,1,0:T(8,128)(2,1)}), bf16[64,16,128]{2,1,0:T(8,128)(2,1)S(1)}, u32[]{:S(2)}, u32[]{:S(2)}) async-start(bf16[64,16,128]{2,1,0:T(8,128)(2,1)} %broadcast_select_fusion.1), calls=%async_computation.4 | async-start | bytes 524288 | tf_op jit(solution)/shard_map/all_to_all | solution.py:19
  251.4 17.9 %all-to-all-start.1 = ((bf16[64,16,128]{2,1,0:T(8,128)(2,1)}), bf16[64,16,128]{2,1,0:T(8,128)(2,1)S(1)}, u32[]{:S(2)}, u32[]{:S(2)}) async-start(bf16[64,16,128]{2,1,0:T(8,128)(2,1)} %broadcast_select_fusion.2), calls=%async_computation.2 | async-start | bytes 524288 | tf_op jit(solution)/shard_map/all_to_all | solution.py:19
  257.3 167.7 %reduce-scatter.8.cloned.1.call-start = ((), (), s32[]{:S(2)}) async-start(), calls=%async_computation.15 | async-start | bytes 1064960 | tf_op jit(solution)/shard_map/reduce_scatter | solution.py:88
  287.8 292.8 %reduce-scatter.10.cloned.1.call-start = ((), (), s32[]{:S(2)}) async-start(), calls=%async_computation.16 | async-start | bytes 8519680
  305.5 1.0 copy-start.2
  309.1 22.7 %all-to-all-start.7 = ((f32[64,16,128]{2,1,0:T(8,128)}), f32[64,16,128]{2,1,0:T(8,128)S(1)}, u32[]{:S(2)}, u32[]{:S(2)}) async-start(f32[64,16,128]{2,1,0:T(8,128)} %bitcast.27), calls=%async_computation.9 | async-start | bytes 1048576 | tf_op jit(solution)/shard_map/all_to_all | solution.py:23
  331.8 23.4 %all-to-all-start.6 = ((f32[64,16,128]{2,1,0:T(8,128)}), f32[64,16,128]{2,1,0:T(8,128)S(1)}, u32[]{:S(2)}, u32[]{:S(2)}) async-start(f32[64,16,128]{2,1,0:T(8,128)} %bitcast.22), calls=%async_computation.8 | async-start | bytes 1048576 | tf_op jit(solution)/shard_map/all_to_all | solution.py:23
  355.2 9.8 %copy-start.3 = (f32[64,16,128]{2,1,0:T(8,128)}, f32[64,16,128]{2,1,0:T(8,128)S(1)}, u32[]{:S(2)}) copy-start(f32[64,16,128]{2,1,0:T(8,128)S(1)} %all-to-all-done.6) | copy-start | bytes 1572868
  355.2 24.8 %all-to-all-start.8 = ((f32[64,16,128]{2,1,0:T(8,128)}), f32[64,16,128]{2,1,0:T(8,128)S(1)}, u32[]{:S(2)}, u32[]{:S(2)}) async-start(f32[64,16,128]{2,1,0:T(8,128)} %bitcast.32), calls=%async_computation.10 | async-start | bytes 1048576 | tf_op jit(solution)/shard_map/all_to_all | solution.py:23
  386.6 194.0 %copy-start.1 = (f32[3072,128]{1,0:T(8,128)}, f32[3072,128]{1,0:T(8,128)S(1)}, u32[]{:S(2)}) copy-start(f32[3072,128]{1,0:T(8,128)S(1)} %scatter_fusion.1) | copy-start | bytes 4718596
Sparse Core Ops, SparseCore 0:
  9.8 52.9 all-gather.2
  65.6 79.9 all-gather.4
  211.5 24.9 reduce-scatter.5
  287.9 137.0 reduce-scatter.7
  429.6 150.8 reduce-scatter.9
where the time goes:
time: 588 us; the launch traced here: 587 us
  waiting for transfers between devices  259 us (44%)
  blocking collectives  144 us (24%)
  starting transfers between devices  77.8 us (13%)
  other arithmetic  37.9 us (6%)
  local copies, waits for them, and re-layouts  35.8 us (6%)
  matrix products  18.3 us (3%)
  between operations  14.2 us (2%)
    unnamed x6, waiting for transfers between devices  157 us
    all_gather x1, blocking collectives, shards(): out_full = lax.all_gather(w_out, ('section', 'dp'), axis=0, tiled=True)  130 us
    reduce_scatter x1, waiting for transfers between devices, shards(): lax.psum_scatter(lax.dot_general(grad_full, hidden, (((0,), (0,)), ((), (...  38.4 us
    all_to_all x3, starting transfers between devices, send_requests(): lax.all_to_all(outgoing, ('section', 'dp'), split_axis=0, concat_axis=0,...  36 us
    all_to_all x3, waiting for transfers between devices, send_sums(): lax.all_to_all(outgoing, ('section', 'dp'), split_axis=0, concat_axis=0,...  29.9 us
    all_to_all x3, waiting for transfers between devices, send_rows(): lax.all_to_all(outgoing, ('section', 'dp'), split_axis=0, concat_axis=0,...  24.3 us
    all_to_all x3, starting transfers between devices, send_rows(): lax.all_to_all(outgoing, ('section', 'dp'), split_axis=0, concat_axis=0,...  22.1 us
    scatter-add x3, other arithmetic, shards(): code_total.at[asked_list[level_index].reshape(-1)]  20.1 us
  transfers between devices with their start and end apart: 14, of which 9 were waited for; matrix products, arithmetic and copies ran while one was open for 15% of the time, Pallas kernels for 0%

commit v1 on v0

--- a/solution.py
+++ b/solution.py
@@ -36,7 +36,12 @@
         preferred_element_type=jnp.float32,
     )
     hidden = jax.nn.silu(preact).astype(jnp.bfloat16)
-    out_full = lax.all_gather(w_out, ("section", "dp"), axis=0, tiled=True)
+    out_full = jnp.concatenate(
+        lax.all_to_all(
+            jnp.stack([w_out] * lax.axis_size(("section", "dp"))), ("section", "dp"), 0, 0
+        ),
+        axis=0,
+    )
     latent_part = lax.dot_general(
         hidden, out_full, (((1,), (1,)), ((), ())), preferred_element_type=jnp.float32
     )

time: 588 us -> 540 us (0.918)
  blocking collectives: 144 us -> 14.5 us
  waiting for transfers between devices: 259 us -> 352 us
  starting transfers between devices: 77.8 us -> 63.7 us
    all_gather x1 -> x0, blocking collectives: 130 us -> none  [shards(): out_full = lax.all_gather(w_out, ('section', 'dp'), axis=0, tiled=True)]
    all_gather x1, waiting for transfers between devices: 0.01 us -> 77.9 us  [shards(): lax.all_gather(w_in, ('section', 'dp'), axis=0, tiled=True)]
    all_to_all x3, waiting for transfers between devices: 9.15 us -> 24.7 us  [send_requests(): lax.all_to_all(outgoing, ('section', 'dp'), split_axis=0, concat_axis=0,...]
    all_to_all x3, starting transfers between devices: 36 us -> 22.9 us  [send_requests(): lax.all_to_all(outgoing, ('section', 'dp'), split_axis=0, concat_axis=0,...]
    unnamed x13 -> x17, local copies, waits for them, and re-layouts: 16.2 us -> 16.2 us
  transfers between devices with their start and end apart: 14 -> 15, of which waited for: 9 -> 12; matrix products, arithmetic and copies ran while one was open for 15% -> 16% of each run, Pallas kernels for 0% -> 0%
where the time goes in v1:
time: 540 us; the launch traced here: 538 us
  waiting for transfers between devices  352 us (65%)
  starting transfers between devices  63.7 us (12%)
  other arithmetic  37.9 us (7%)
  local copies, waits for them, and re-layouts  37.4 us (7%)
  matrix products  18.3 us (3%)
  blocking collectives  14.5 us (3%)
  between operations  14.3 us (3%)
    unnamed x6, waiting for transfers between devices  157 us
    all_gather x1, waiting for transfers between devices, shards(): lax.all_gather(w_in, ('section', 'dp'), axis=0, tiled=True)  77.9 us
    reduce_scatter x1, waiting for transfers between devices, shards(): lax.psum_scatter(lax.dot_general(grad_full, hidden, (((0,), (0,)), ((), (...  38.5 us
    all_to_all x3, waiting for transfers between devices, send_sums(): lax.all_to_all(outgoing, ('section', 'dp'), split_axis=0, concat_axis=0,...  30.1 us
    all_to_all x3, waiting for transfers between devices, send_requests(): lax.all_to_all(outgoing, ('section', 'dp'), split_axis=0, concat_axis=0,...  24.7 us
    all_to_all x3, waiting for transfers between devices, send_rows(): lax.all_to_all(outgoing, ('section', 'dp'), split_axis=0, concat_axis=0,...  24.4 us
    all_to_all x3, starting transfers between devices, send_requests(): lax.all_to_all(outgoing, ('section', 'dp'), split_axis=0, concat_axis=0,...  22.9 us
    scatter-add x3, other arithmetic, shards(): code_total.at[asked_list[level_index].reshape(-1)]  20.1 us
  transfers between devices with their start and end apart: 15, of which 12 were waited for; matrix products, arithmetic and copies ran while one was open for 16% of the time, Pallas kernels for 0%

profile of v1, /device:TPU:8, one launch (start us, length us, event | category | flops | bytes accessed | tf_op | source)
XLA Modules:
  0.0 538.5 jit_solution(9360464335784851724)
XLA Ops:
  9.5 3.6 reduce-window.6
  15.3 6.2 %scatter_custom_fusion.6 = s32[3072]{0:T(1024)S(1)} fusion(s32[1536]{0:T(1024)S(1)} %reshape.383, s32[1536]{0:T(1024)S(1)} %reshape.385, s32[]{:T(128)} %constant.45.clone.1), kind=kCustom, calls=%fused_computation.75 | custom fusion | bytes 12292
  22.2 11.9 %all-to-all-start.5 = ((s32[64,1,16]{2,1,0:T(1,128)}), s32[64,1,16]{2,1,0:T(1,128)S(1)}, u32[]{:S(2)}, u32[]{:S(2)}) async-start(s32[64,1,16]{2,1,0:T(1,128)} %bitcast.15), calls=%async_computation.6 | async-start | bytes 65536 | tf_op jit(solution)/shard_map/all_to_all | solution.py:15
  35.6 7.8 %all-to-all-done.5 = s32[64,1,16]{2,1,0:T(1,128)S(1)} async-done(((s32[64,1,16]{2,1,0:T(1,128)}), s32[64,1,16]{2,1,0:T(1,128)S(1)}, u32[]{:S(2)}, u32[]{:S(2)}) %all-to-all-start.5) | async-done | bytes 4128 | tf_op jit(solution)/shard_map/all_to_all | solution.py:15
  43.4 4.6 all-to-all-start.3
  48.1 9.1 %all-to-all-done.3 = s32[64,1,16]{2,1,0:T(1,128)S(1)} async-done(((s32[64,1,16]{2,1,0:T(1,128)}), s32[64,1,16]{2,1,0:T(1,128)S(1)}, u32[]{:S(2)}, u32[]{:S(2)}) %all-to-all-start.3) | async-done | bytes 4128 | tf_op jit(solution)/shard_map/all_to_all | solution.py:15
  58.8 4.6 all-to-all-start
  63.5 3.2 gather_fusion.4
  67.6 77.9 %all-gather.5.cloned.1.call-done = bf16[4096,512]{1,0:T(8,128)(2,1)} async-done(((bf16[64,512]{1,0:T(8,128)(2,1)}), bf16[4096,512]{1,0:T(8,128)(2,1)}) %all-gather.5.cloned.1.call-update) | async-done | bytes 4194320 | tf_op jit(solution)/shard_map/all_gather | solution.py:35
  145.5 5.8 %fusion.30 = f32[512,512]{1,0:T(8,128)S(1)} fusion(bf16[512,4096]{1,0:T(8,128)(2,1)} %all-gather.3.cloned.1.call-done, bf16[4096,512]{1,0:T(8,128)(2,1)} %all-gather.5.cloned.1.call-done), kind=kOutput, calls=%fused_computation.96 | convolution fusion | flops 2147483648 | bytes 9437184 | tf_op jit(solution)/shard_map/dot_general | solution.py:33
  151.3 6.3 %all-to-all-start.1 = ((s32[64,1,16]{2,1,0:T(1,128)}), s32[64,1,16]{2,1,0:T(1,128)S(1)}, u32[]{:S(2)}, u32[]{:S(2)}) async-start(s32[64,1,16]{2,1,0:T(1,128)} %bitcast.4), calls=%async_computation.2 | async-start | bytes 65536 | tf_op jit(solution)/shard_map/all_to_all | solution.py:15
  159.2 7.8 %all-to-all-done.1 = s32[64,1,16]{2,1,0:T(1,128)S(1)} async-done(((s32[64,1,16]{2,1,0:T(1,128)}), s32[64,1,16]{2,1,0:T(1,128)S(1)}, u32[]{:S(2)}, u32[]{:S(2)}) %all-to-all-start.1) | async-done | bytes 4128 | tf_op jit(solution)/shard_map/all_to_all | solution.py:15
  167.0 4.6 all-to-all-start.6
  175.9 7.6 %all-to-all-done.6 = bf16[64,16,128]{2,1,0:T(8,128)(2,1)S(1)} async-done(((bf16[64,16,128]{2,1,0:T(8,128)(2,1)}), bf16[64,16,128]{2,1,0:T(8,128)(2,1)S(1)}, u32[]{:S(2)}, u32[]{:S(2)}) %all-to-all-start.6) | async-done | bytes 262176 | tf_op jit(solution)/shard_map/all_to_all | solution.py:19
  183.5 6.0 %all-to-all-start.4 = ((bf16[64,16,128]{2,1,0:T(8,128)(2,1)}), bf16[64,16,128]{2,1,0:T(8,128)(2,1)S(1)}, u32[]{:S(2)}, u32[]{:S(2)}) async-start(bf16[64,16,128]{2,1,0:T(8,128)(2,1)} %broadcast_select_fusion.1), calls=%async_computation.5 | async-start | bytes 524288 | tf_op jit(solution)/shard_map/all_to_all | solution.py:19
  189.5 3.2 gather_fusion
  193.7 7.7 %all-to-all-done.4 = bf16[64,16,128]{2,1,0:T(8,128)(2,1)S(1)} async-done(((bf16[64,16,128]{2,1,0:T(8,128)(2,1)}), bf16[64,16,128]{2,1,0:T(8,128)(2,1)S(1)}, u32[]{:S(2)}, u32[]{:S(2)}) %all-to-all-start.4) | async-done | bytes 262176 | tf_op jit(solution)/shard_map/all_to_all | solution.py:19
  201.4 6.0 %all-to-all-start.2 = ((bf16[64,16,128]{2,1,0:T(8,128)(2,1)}), bf16[64,16,128]{2,1,0:T(8,128)(2,1)S(1)}, u32[]{:S(2)}, u32[]{:S(2)}) async-start(bf16[64,16,128]{2,1,0:T(8,128)(2,1)} %broadcast_select_fusion.2), calls=%async_computation.3 | async-start | bytes 524288 | tf_op jit(solution)/shard_map/all_to_all | solution.py:19
  210.1 9.1 %all-to-all-done.2 = bf16[64,16,128]{2,1,0:T(8,128)(2,1)S(1)} async-done(((bf16[64,16,128]{2,1,0:T(8,128)(2,1)}), bf16[64,16,128]{2,1,0:T(8,128)(2,1)S(1)}, u32[]{:S(2)}, u32[]{:S(2)}) %all-to-all-start.2) | async-done | bytes 262176 | tf_op jit(solution)/shard_map/all_to_all | solution.py:19
  221.9 14.5 %all_gather.11 = bf16[512,512]{1,0:T(8,128)(2,1)S(1)} all-gather(bf16[512,128]{1,0:T(8,128)(2,1)S(1)} %multiply_convert_fusion.1), channel_id=1, replica_groups=mesh['section'=2,'dp'=32,'mp'=4] {'mp'}, dimensions={1}, use_global_device_ids=true | all-gather | bytes 655360 | tf_op jit(solution)/shard_map/all_gather | solution.py:92
  239.2 8.3 %convolution_bitcast_fusion = f32[4096,512]{0,1:T(8,128)} fusion(bf16[512,4096]{1,0:T(8,128)(2,1)} %all-gather.3.cloned.1.call-done, bf16[512,512]{1,0:T(8,128)(2,1)S(1)} %all_gather.11, f32[512,512]{1,0:T(8,128)S(1)} %copy-done.6, bf16[64,8,512]{2,1,0:T(8,128)(2,1)S(1)} %all-to-all-done), kind=kOutput, calls=%fused_computation.13 | convolution fusion | flops 2418278400 | bytes 14680064 | tf_op jit(solution)/shard_map/dot_general | solution.py:104
  247.5 9.0 %copy.17 = f32[4096,512]{1,0:T(8,128)} copy(f32[4096,512]{0,1:T(8,128)} %convolution_bitcast_fusion) | data formatting | bytes 16777216
  260.1 6.1 %all-to-all-start.8 = ((f32[64,16,128]{2,1,0:T(8,128)}), f32[64,16,128]{2,1,0:T(8,128)S(1)}, u32[]{:S(2)}, u32[]{:S(2)}) async-start(f32[64,16,128]{2,1,0:T(8,128)} %bitcast.28), calls=%async_computation.10 | async-start | bytes 1048576 | tf_op jit(solution)/shard_map/all_to_all | solution.py:23
  268.8 14.3 %all-to-all-done.8 = f32[64,16,128]{2,1,0:T(8,128)S(1)} async-done(((f32[64,16,128]{2,1,0:T(8,128)}), f32[64,16,128]{2,1,0:T(8,128)S(1)}, u32[]{:S(2)}, u32[]{:S(2)}) %all-to-all-start.8) | async-done | bytes 524320 | tf_op jit(solution)/shard_map/all_to_all | solution.py:23
  283.1 6.6 %all-to-all-start.7 = ((f32[64,16,128]{2,1,0:T(8,128)}), f32[64,16,128]{2,1,0:T(8,128)S(1)}, u32[]{:S(2)}, u32[]{:S(2)}) async-start(f32[64,16,128]{2,1,0:T(8,128)} %bitcast.23), calls=%async_computation.9 | async-start | bytes 1048576 | tf_op jit(solution)/shard_map/all_to_all | solution.py:23
  292.4 14.1 %all-to-all-done.7 = f32[64,16,128]{2,1,0:T(8,128)S(1)} async-done(((f32[64,16,128]{2,1,0:T(8,128)}), f32[64,16,128]{2,1,0:T(8,128)S(1)}, u32[]{:S(2)}, u32[]{:S(2)}) %all-to-all-start.7) | async-done | bytes 524320 | tf_op jit(solution)/shard_map/all_to_all | solution.py:23
  306.5 6.8 %all-to-all-start.9 = ((f32[64,16,128]{2,1,0:T(8,128)}), f32[64,16,128]{2,1,0:T(8,128)S(1)}, u32[]{:S(2)}, u32[]{:S(2)}) async-start(f32[64,16,128]{2,1,0:T(8,128)} %bitcast.33), calls=%async_computation.11 | async-start | bytes 1048576 | tf_op jit(solution)/shard_map/all_to_all | solution.py:23
  316.3 6.8 %scatter_custom_fusion.1 = f32[3072,128]{1,0:T(8,128)S(1)} fusion(s32[1024]{0:T(1024)S(1)} %bitcast.97, f32[1024,128]{1,0:T(8,128)} %bitcast.82, f32[]{:T(128)} %constant.79.clone.1), kind=kCustom, calls=%fused_computation.22 | custom fusion | flops 131072 | bytes 1573376 | tf_op jit(solution)/shard_map/scatter-add | solution.py:84
  323.1 6.6 %scatter_fusion = f32[3072,128]{1,0:T(8,128)S(1)} fusion(f32[3072,128]{1,0:T(8,128)S(1)} %scatter_custom_fusion.1, s32[1024]{0:T(1024)S(1)} %bitcast.96, f32[1024,128]{1,0:T(8,128)S(1)} %bitcast.77), kind=kCustom, calls=%fused_computation.9 | custom fusion | flops 131072 | bytes 1576960 | tf_op jit(solution)/shard_map/scatter-add | solution.py:84
  331.4 6.6 %scatter_fusion.1 = f32[3072,128]{1,0:T(8,128)S(1)} fusion(f32[3072,128]{1,0:T(8,128)S(1)} %scatter_fusion, s32[1024]{0:T(1024)S(1)} %bitcast.95, f32[1024,128]{1,0:T(8,128)S(1)} %bitcast.78), kind=kCustom, calls=%fused_computation.11 | custom fusion | flops 131072 | bytes 1576960 | tf_op jit(solution)/shard_map/scatter-add | solution.py:84
  338.1 38.5 %reduce-scatter.8.cloned.1.call-done = f32[8,512]{1,0:T(8,128)} async-done(((f32[512,512]{1,0:T(8,128)}), f32[8,512]{1,0:T(8,128)}) %reduce-scatter.8.cloned.1.call-update) | async-done | bytes 16400 | tf_op jit(solution)/shard_map/reduce_scatter | solution.py:93
  376.5 155.4 %reduce-scatter.10.cloned.1.call-done = f32[64,512]{1,0:T(8,128)} async-done(((f32[4096,512]{1,0:T(8,128)}), f32[64,512]{1,0:T(8,128)}) %reduce-scatter.10.cloned.1.call-update) | async-done | bytes 131088
  (93 shorter events, 37.5 us)
Async XLA Ops:
  7.2 56.3 %copy-start = (bf16[3,1024,128]{2,1,0:T(8,128)(2,1)S(1)}, bf16[3,1024,128]{2,1,0:T(8,128)(2,1)}, u32[]{:S(2)}) copy-start(bf16[3,1024,128]{2,1,0:T(8,128)(2,1)} %param.13) | copy-start | bytes 2359300
  7.2 60.5 %all-gather.3.cloned.1.call-start = ((), (), s32[]{:S(2)}) async-start(), calls=%async_computation.13 | async-start | bytes 5242880 | tf_op jit(solution)/shard_map/all_gather | solution.py:32
  7.9 137.6 %all-gather.5.cloned.1.call-start = ((), (), s32[]{:S(2)}) async-start(), calls=%async_computation.14 | async-start | bytes 4259840 | tf_op jit(solution)/shard_map/all_gather | solution.py:35
  22.2 21.2 %all-to-all-start.5 = ((s32[64,1,16]{2,1,0:T(1,128)}), s32[64,1,16]{2,1,0:T(1,128)S(1)}, u32[]{:S(2)}, u32[]{:S(2)}) async-start(s32[64,1,16]{2,1,0:T(1,128)} %bitcast.15), calls=%async_computation.6 | async-start | bytes 65536 | tf_op jit(solution)/shard_map/all_to_all | solution.py:15
  43.4 13.8 %all-to-all-start.3 = ((s32[64,1,16]{2,1,0:T(1,128)}), s32[64,1,16]{2,1,0:T(1,128)S(1)}, u32[]{:S(2)}, u32[]{:S(2)}) async-start(s32[64,1,16]{2,1,0:T(1,128)} %bitcast.10), calls=%async_computation.4 | async-start | bytes 65536 | tf_op jit(solution)/shard_map/all_to_all | solution.py:15
  58.8 92.6 %all-to-all-start = ((bf16[64,8,512]{2,1,0:T(8,128)(2,1)}), bf16[64,8,512]{2,1,0:T(8,128)(2,1)S(1)}, u32[]{:S(2)}, u32[]{:S(2)}) async-start(bf16[64,8,512]{2,1,0:T(8,128)(2,1)} %stack.2), calls=%async_computation | async-start | bytes 1048576 | tf_op jit(solution)/shard_map/all_to_all | solution.py:40
  151.3 15.7 %copy-start.5 = (f32[512,512]{1,0:T(8,128)}, f32[512,512]{1,0:T(8,128)S(1)}, u32[]{:S(2)}) copy-start(f32[512,512]{1,0:T(8,128)S(1)} %fusion.30) | copy-start | bytes 3145732
  151.3 15.6 %all-to-all-start.1 = ((s32[64,1,16]{2,1,0:T(1,128)}), s32[64,1,16]{2,1,0:T(1,128)S(1)}, u32[]{:S(2)}, u32[]{:S(2)}) async-start(s32[64,1,16]{2,1,0:T(1,128)} %bitcast.4), calls=%async_computation.2 | async-start | bytes 65536 | tf_op jit(solution)/shard_map/all_to_all | solution.py:15
  157.7 62.9 %reduce-scatter.6.cloned.1.call-start = ((), (), s32[]{:S(2)}) async-start(), calls=%async_computation.15 | async-start | bytes 1310720 | tf_op jit(solution)/shard_map/reduce_scatter | solution.py:48
  167.0 16.5 %all-to-all-start.6 = ((bf16[64,16,128]{2,1,0:T(8,128)(2,1)}), bf16[64,16,128]{2,1,0:T(8,128)(2,1)S(1)}, u32[]{:S(2)}, u32[]{:S(2)}) async-start(bf16[64,16,128]{2,1,0:T(8,128)(2,1)} %broadcast_select_fusion), calls=%async_computation.7 | async-start | bytes 524288 | tf_op jit(solution)/shard_map/all_to_all | solution.py:19
  174.9 45.7 %copy-start.4 = (bf16[512,128]{1,0:T(8,128)(2,1)S(1)}, bf16[512,128]{1,0:T(8,128)(2,1)}, u32[]{:S(2)}) copy-start(bf16[512,128]{1,0:T(8,128)(2,1)} %param.15) | copy-start | bytes 393220
  183.5 17.9 %all-to-all-start.4 = ((bf16[64,16,128]{2,1,0:T(8,128)(2,1)}), bf16[64,16,128]{2,1,0:T(8,128)(2,1)S(1)}, u32[]{:S(2)}, u32[]{:S(2)}) async-start(bf16[64,16,128]{2,1,0:T(8,128)(2,1)} %broadcast_select_fusion.1), calls=%async_computation.5 | async-start | bytes 524288 | tf_op jit(solution)/shard_map/all_to_all | solution.py:19
  201.4 17.9 %all-to-all-start.2 = ((bf16[64,16,128]{2,1,0:T(8,128)(2,1)}), bf16[64,16,128]{2,1,0:T(8,128)(2,1)S(1)}, u32[]{:S(2)}, u32[]{:S(2)}) async-start(bf16[64,16,128]{2,1,0:T(8,128)(2,1)} %broadcast_select_fusion.2), calls=%async_computation.3 | async-start | bytes 524288 | tf_op jit(solution)/shard_map/all_to_all | solution.py:19
  207.4 169.2 %reduce-scatter.8.cloned.1.call-start = ((), (), s32[]{:S(2)}) async-start(), calls=%async_computation.16 | async-start | bytes 1064960 | tf_op jit(solution)/shard_map/reduce_scatter | solution.py:93
  221.9 17.3 %copy-start.6 = (f32[512,512]{1,0:T(8,128)S(1)}, f32[512,512]{1,0:T(8,128)}, u32[]{:S(2)}) copy-start(f32[512,512]{1,0:T(8,128)} %copy-done.5) | copy-start | bytes 3145732
  239.2 292.8 %reduce-scatter.10.cloned.1.call-start = ((), (), s32[]{:S(2)}) async-start(), calls=%async_computation.17 | async-start | bytes 8519680
  256.5 1.0 copy-start.2
  260.1 22.9 %all-to-all-start.8 = ((f32[64,16,128]{2,1,0:T(8,128)}), f32[64,16,128]{2,1,0:T(8,128)S(1)}, u32[]{:S(2)}, u32[]{:S(2)}) async-start(f32[64,16,128]{2,1,0:T(8,128)} %bitcast.28), calls=%async_computation.10 | async-start | bytes 1048576 | tf_op jit(solution)/shard_map/all_to_all | solution.py:23
  283.1 23.4 %all-to-all-start.7 = ((f32[64,16,128]{2,1,0:T(8,128)}), f32[64,16,128]{2,1,0:T(8,128)S(1)}, u32[]{:S(2)}, u32[]{:S(2)}) async-start(f32[64,16,128]{2,1,0:T(8,128)} %bitcast.23), calls=%async_computation.9 | async-start | bytes 1048576 | tf_op jit(solution)/shard_map/all_to_all | solution.py:23
  306.5 9.8 %copy-start.3 = (f32[64,16,128]{2,1,0:T(8,128)}, f32[64,16,128]{2,1,0:T(8,128)S(1)}, u32[]{:S(2)}) copy-start(f32[64,16,128]{2,1,0:T(8,128)S(1)} %all-to-all-done.7) | copy-start | bytes 1572868
  306.5 25.0 %all-to-all-start.9 = ((f32[64,16,128]{2,1,0:T(8,128)}), f32[64,16,128]{2,1,0:T(8,128)S(1)}, u32[]{:S(2)}, u32[]{:S(2)}) async-start(f32[64,16,128]{2,1,0:T(8,128)} %bitcast.33), calls=%async_computation.11 | async-start | bytes 1048576 | tf_op jit(solution)/shard_map/all_to_all | solution.py:23
  338.1 193.9 %copy-start.1 = (f32[3072,128]{1,0:T(8,128)}, f32[3072,128]{1,0:T(8,128)S(1)}, u32[]{:S(2)}) copy-start(f32[3072,128]{1,0:T(8,128)S(1)} %scatter_fusion.1) | copy-start | bytes 4718596
Sparse Core Ops, SparseCore 0:
  9.8 53.0 all-gather.2
  65.6 79.8 all-gather.4
  161.6 24.8 reduce-scatter.5
  239.3 137.2 reduce-scatter.7
  381.2 150.7 reduce-scatter.9
